TPU v7x, 128 devices: a whole 4x4x4 slice. The times are simulated.
128 devices in a mesh: wide: 16 (over z_hi, x, core), narrow: 8 (over z_lo, y).
Axes of the slice: x: 4, y: 4, z: 4 (z_hi: 2, z_lo: 2; z = z_hi * 2 + z_lo), core: 2. Of those that a mesh axis runs over, the one named last changes fastest.
Arguments:
- tokens: bfloat16 [12288, 1024], P(('wide', 'narrow')), may hold values from -6 to 6
- cotangent: bfloat16 [12288, 1024], P(('wide', 'narrow')), may hold values from -6 to 6
- segments: int32 [16, 768], P('wide'), may hold values from 0 to 3, never falling along the last dimension, each value on 1 to 384 neighbouring positions
- w_query: bfloat16 [1024, 1024], P(None, 'narrow'), may hold values from -0.1875 to 0.1875
- w_key: bfloat16 [1024, 1024], P(None, 'narrow'), may hold values from -0.1875 to 0.1875
- w_value: bfloat16 [1024, 1024], P(None, 'narrow'), may hold values from -0.1875 to 0.1875
- w_out: bfloat16 [1024, 1024], P('narrow'), may hold values from -1.5 to 1.5
- w_gate: bfloat16 [1024, 4096], P(None, 'narrow'), may hold values from -0.1875 to 0.1875
- w_up: bfloat16 [1024, 4096], P(None, 'narrow'), may hold values from -0.1875 to 0.1875
- w_down: bfloat16 [4096, 1024], P('narrow'), may hold values from -0.09375 to 0.09375
- gain_one: float32 [1024], replicated, may hold values from 0.25 to 1.75
- bias_one: float32 [1024], replicated, may hold values from -2.5 to 2.5
- gain_two: float32 [1024], replicated, may hold values from 0.25 to 1.75
- bias_two: float32 [1024], replicated, may hold values from -2.5 to 2.5
Outputs:
- layer_out: float32 [12288, 1024], P(('wide', 'narrow'))
- input_grad: float32 [12288, 1024], P(('wide', 'narrow'))
- grad_query: float32 [1024, 1024], P(None, 'narrow')
- grad_key: float32 [1024, 1024], P(None, 'narrow')
- grad_value: float32 [1024, 1024], P(None, 'narrow')
- grad_out: float32 [1024, 1024], P('narrow')
- grad_gate: float32 [1024, 4096], P(None, 'narrow')
- grad_up: float32 [1024, 4096], P(None, 'narrow')
- grad_down: float32 [4096, 1024], P('narrow')
- grad_gain_one: float32 [1024], replicated
- grad_bias_one: float32 [1024], replicated
- grad_gain_two: float32 [1024], replicated
- grad_bias_two: float32 [1024], replicated
Inputs may be any that keep to these rules, and one draw needn't show every extreme that they name: `segments`: within each row of 768 tokens segment numbers never fall; each segment holds 1 to 384 tokens and one holds exactly 384.
All inputs are finite; a program needn't handle non-finite values.
Results may differ from a plain program's by a relative error of at most 0.03.
Values may be sent and summed in bfloat16 or wider, within the bound.
No kernel may reach another device: no remote copies, remote signals or barrier semaphores. Data moves between devices by JAX's collectives and lax.ppermute only.
A program may use at most 128 MiB of HBM per device.

v0:
```python
import math
import jax
import jax.numpy as jnp
from jax import lax
from jax.sharding import PartitionSpec as P

HD = 64
EPS = 1e-05
MASKED = -1e30


def normalize(values, gain_vec, bias_vec):
    centred = values - jnp.mean(values, axis=-1, keepdims=True)
    inverse = lax.rsqrt(jnp.mean(centred * centred, axis=-1, keepdims=True) + EPS)
    scaled = centred * inverse
    return (scaled * gain_vec + bias_vec, scaled, inverse)


def normalize_back(grad_in, scaled, inverse, gain_vec):
    along = grad_in * gain_vec
    return inverse * (
        along
        - jnp.mean(along, axis=-1, keepdims=True)
        - scaled * jnp.mean(along * scaled, axis=-1, keepdims=True)
    )


def contract_last(left_side, right_side):
    return lax.dot_general(
        left_side, right_side, (((1,), (1,)), ((), ())), preferred_element_type=jnp.float32
    )


def contract_first(left_side, right_side):
    return lax.dot_general(
        left_side, right_side, (((0,), (0,)), ((), ())), preferred_element_type=jnp.float32
    )


def rotary_tables(seg_rows):
    length = seg_rows.shape[-1]
    column = lax.broadcasted_iota(jnp.int32, (length, length), 1)
    row_index = lax.broadcasted_iota(jnp.int32, (length,), 0)
    same_segment = seg_rows[..., :, None] == seg_rows[..., None, :]
    first_index = jnp.min(jnp.where(same_segment, column, length), axis=-1)
    position = (row_index - first_index).astype(jnp.float32)
    half_width = HD // 2
    inverse = 10000.0 ** (-(2.0 * jnp.arange(half_width).astype(jnp.float32) / HD))
    angles = position[..., None] * inverse
    return (jnp.cos(angles), jnp.sin(angles), same_segment)


def rotate(values, cosine_table, sine_table):
    half_width = values.shape[-1] // 2
    first_half = values[..., :half_width]
    second_half = values[..., half_width:]
    cosine = cosine_table[..., None, :]
    sine_part = sine_table[..., None, :]
    return jnp.concatenate(
        [
            first_half * cosine - second_half * sine_part,
            second_half * cosine + first_half * sine_part,
        ],
        axis=-1,
    )


def unrotate(values, cosine_table, sine_table):
    half_width = values.shape[-1] // 2
    first_half = values[..., :half_width]
    second_half = values[..., half_width:]
    cosine = cosine_table[..., None, :]
    sine_part = sine_table[..., None, :]
    return jnp.concatenate(
        [
            first_half * cosine + second_half * sine_part,
            second_half * cosine - first_half * sine_part,
        ],
        axis=-1,
    )


def project_heads(normed_one, w_query, w_key, w_value, cosine_table, sine_table):
    row_count, length = (cosine_table.shape[0], cosine_table.shape[1])
    head_shape = (row_count, length, w_query.shape[1] // HD, HD)
    queries = rotate(
        jnp.dot(normed_one, w_query, preferred_element_type=jnp.float32).reshape(head_shape),
        cosine_table,
        sine_table,
    ).astype(jnp.bfloat16)
    key_rows = rotate(
        jnp.dot(normed_one, w_key, preferred_element_type=jnp.float32).reshape(head_shape),
        cosine_table,
        sine_table,
    ).astype(jnp.bfloat16)
    value_rows = (
        jnp.dot(normed_one, w_value, preferred_element_type=jnp.float32)
        .astype(jnp.bfloat16)
        .reshape(head_shape)
    )
    return (queries, key_rows, value_rows)


def attention_forward(normed_one, w_query, w_key, w_value, cosine_table, sine_table, same_segment):
    queries, key_rows, value_rows = project_heads(
        normed_one, w_query, w_key, w_value, cosine_table, sine_table
    )
    score_scale = 1.0 / math.sqrt(HD)

    def one_row(row_items):
        query_row, key_row, value_row, mask_row = row_items
        scores = (
            jnp.einsum("qhd,khd->hqk", query_row, key_row, preferred_element_type=jnp.float32)
            * score_scale
        )
        scores = jnp.where(mask_row[None], scores, MASKED)
        row_peak = jnp.max(scores, axis=-1, keepdims=True)
        exponent = jnp.exp(scores - row_peak)
        row_total = jnp.sum(exponent, axis=-1, keepdims=True)
        probs_low = (exponent / row_total).astype(jnp.bfloat16)
        output = jnp.einsum(
            "hqk,khd->qhd", probs_low, value_row, preferred_element_type=jnp.float32
        ).astype(jnp.bfloat16)
        return (output, row_peak + jnp.log(row_total))

    attended, log_total = lax.map(one_row, (queries, key_rows, value_rows, same_segment))
    return (attended.reshape(normed_one.shape[0], -1), log_total)


def attention_grads(
    normed_one,
    attended,
    log_total,
    branch_grad,
    w_query,
    w_key,
    w_value,
    w_out,
    cosine_table,
    sine_table,
    same_segment,
):
    queries, key_rows, value_rows = project_heads(
        normed_one, w_query, w_key, w_value, cosine_table, sine_table
    )
    score_scale = 1.0 / math.sqrt(HD)
    grad_out = contract_first(attended, branch_grad)
    attended_grad = contract_last(branch_grad, w_out).astype(jnp.bfloat16).reshape(queries.shape)

    def one_row(row_items):
        query_row, key_row, value_row, mask_row, total_row, grad_row = row_items
        scores = (
            jnp.einsum("qhd,khd->hqk", query_row, key_row, preferred_element_type=jnp.float32)
            * score_scale
        )
        scores = jnp.where(mask_row[None], scores, MASKED)
        probs = jnp.exp(scores - total_row)
        probs_low = probs.astype(jnp.bfloat16)
        prob_grad = jnp.einsum(
            "qhd,khd->hqk", grad_row, value_row, preferred_element_type=jnp.float32
        )
        score_grad = (
            probs * (prob_grad - jnp.sum(probs * prob_grad, axis=-1, keepdims=True))
        ).astype(jnp.bfloat16)
        query_grad = score_scale * jnp.einsum(
            "hqk,khd->qhd", score_grad, key_row, preferred_element_type=jnp.float32
        )
        key_grad = score_scale * jnp.einsum(
            "hqk,qhd->khd", score_grad, query_row, preferred_element_type=jnp.float32
        )
        value_grad = jnp.einsum(
            "hqk,qhd->khd", probs_low, grad_row, preferred_element_type=jnp.float32
        ).astype(jnp.bfloat16)
        return (query_grad, key_grad, value_grad)

    query_grad, key_grad, value_grad = lax.map(
        one_row, (queries, key_rows, value_rows, same_segment, log_total, attended_grad)
    )
    token_count = normed_one.shape[0]
    query_grad = (
        unrotate(query_grad, cosine_table, sine_table).astype(jnp.bfloat16).reshape(token_count, -1)
    )
    key_grad = (
        unrotate(key_grad, cosine_table, sine_table).astype(jnp.bfloat16).reshape(token_count, -1)
    )
    value_grad = value_grad.reshape(token_count, -1)
    grad_query = contract_first(normed_one, query_grad)
    grad_key = contract_first(normed_one, key_grad)
    grad_value = contract_first(normed_one, value_grad)
    partial_sum = (
        contract_last(query_grad, w_query)
        + contract_last(key_grad, w_key)
        + contract_last(value_grad, w_value)
    )
    return (partial_sum, grad_query, grad_key, grad_value, grad_out)


def swiglu(normed_two, w_gate, w_up):
    gate_pre = jnp.dot(normed_two, w_gate, preferred_element_type=jnp.float32)
    up_pre = jnp.dot(normed_two, w_up, preferred_element_type=jnp.float32)
    sigmoid_gate = jax.nn.sigmoid(gate_pre)
    active = gate_pre * sigmoid_gate
    hidden = (active * up_pre).astype(jnp.bfloat16)
    return (hidden, gate_pre, up_pre, sigmoid_gate, active)


def swiglu_grads(normed_two, out_grad, w_gate, w_up, w_down):
    hidden, gate_pre, up_pre, sigmoid_gate, active = swiglu(normed_two, w_gate, w_up)
    hidden_grad = contract_last(out_grad, w_down)
    grad_down = contract_first(hidden, out_grad)
    gate_grad = (
        hidden_grad * up_pre * sigmoid_gate * (1.0 + gate_pre * (1.0 - sigmoid_gate))
    ).astype(jnp.bfloat16)
    up_grad = (hidden_grad * active).astype(jnp.bfloat16)
    grad_gate = contract_first(normed_two, gate_grad)
    grad_up = contract_first(normed_two, up_grad)
    partial_sum = contract_last(gate_grad, w_gate) + contract_last(up_grad, w_up)
    return (partial_sum, grad_gate, grad_up, grad_down)


def per_device(
    tokens,
    cotangent,
    segments,
    w_query,
    w_key,
    w_value,
    w_out,
    w_gate,
    w_up,
    w_down,
    gain_one,
    bias_one,
    gain_two,
    bias_two,
):
    shard_rows = tokens.shape[0]
    narrow_index = lax.axis_index("narrow")
    cosine_table, sine_table, same_segment = rotary_tables(segments)
    gathered, cot_whole = (
        lax.all_gather(tokens, "narrow", axis=0, tiled=True),
        lax.all_gather(cotangent, "narrow", axis=0, tiled=True),
    )
    inputs = gathered.astype(jnp.float32)
    normed_float, scaled_one, inverse_one = normalize(inputs, gain_one, bias_one)
    normed_one = normed_float.astype(jnp.bfloat16)
    attended, log_total = attention_forward(
        normed_one, w_query, w_key, w_value, cosine_table, sine_table, same_segment
    )
    middle = inputs + lax.psum(
        jnp.dot(attended, w_out, preferred_element_type=jnp.float32).astype(jnp.bfloat16), "narrow"
    ).astype(jnp.float32)
    normed_float_two, scaled_two, inverse_two = normalize(middle, gain_two, bias_two)
    normed_two = normed_float_two.astype(jnp.bfloat16)
    hidden = swiglu(normed_two, w_gate, w_up)[0]
    result_whole = middle + lax.psum(
        jnp.dot(hidden, w_down, preferred_element_type=jnp.float32).astype(jnp.bfloat16), "narrow"
    ).astype(jnp.float32)
    layer_out = lax.dynamic_slice_in_dim(result_whole, narrow_index * shard_rows, shard_rows, 0)
    partial_two, grad_gate, grad_up, grad_down = swiglu_grads(
        normed_two, cot_whole, w_gate, w_up, w_down
    )
    normed_two_grad = lax.psum(partial_two.astype(jnp.bfloat16), "narrow").astype(jnp.float32)
    middle_grad = cot_whole.astype(jnp.float32) + normalize_back(
        normed_two_grad, scaled_two, inverse_two, gain_two
    )
    own_two_grad = lax.dynamic_slice_in_dim(
        normed_two_grad, narrow_index * shard_rows, shard_rows, 0
    )
    own_scaled_two = lax.dynamic_slice_in_dim(scaled_two, narrow_index * shard_rows, shard_rows, 0)
    branch_grad = middle_grad.astype(jnp.bfloat16)
    partial_one, grad_query, grad_key, grad_value, grad_out = attention_grads(
        normed_one,
        attended,
        log_total,
        branch_grad,
        w_query,
        w_key,
        w_value,
        w_out,
        cosine_table,
        sine_table,
        same_segment,
    )
    normed_one_grad = lax.psum(partial_one.astype(jnp.bfloat16), "narrow").astype(jnp.float32)
    input_whole = middle_grad + normalize_back(normed_one_grad, scaled_one, inverse_one, gain_one)
    input_grad = lax.dynamic_slice_in_dim(input_whole, narrow_index * shard_rows, shard_rows, 0)
    own_one_grad = lax.dynamic_slice_in_dim(
        normed_one_grad, narrow_index * shard_rows, shard_rows, 0
    )
    own_scaled_one = lax.dynamic_slice_in_dim(scaled_one, narrow_index * shard_rows, shard_rows, 0)
    matrices = (
        lax.psum(grad_query.astype(jnp.bfloat16), "wide").astype(jnp.float32),
        lax.psum(grad_key.astype(jnp.bfloat16), "wide").astype(jnp.float32),
        lax.psum(grad_value.astype(jnp.bfloat16), "wide").astype(jnp.float32),
        lax.psum(grad_out.astype(jnp.bfloat16), "wide").astype(jnp.float32),
        lax.psum(grad_gate.astype(jnp.bfloat16), "wide").astype(jnp.float32),
        lax.psum(grad_up.astype(jnp.bfloat16), "wide").astype(jnp.float32),
        lax.psum(grad_down.astype(jnp.bfloat16), "wide").astype(jnp.float32),
    )
    norm_grads = lax.psum(
        (
            jnp.sum(own_one_grad * own_scaled_one, axis=0),
            jnp.sum(own_one_grad, axis=0),
            jnp.sum(own_two_grad * own_scaled_two, axis=0),
            jnp.sum(own_two_grad, axis=0),
        ),
        ("wide", "narrow"),
    )
    return (
        layer_out,
        input_grad,
        matrices[0],
        matrices[1],
        matrices[2],
        matrices[3],
        matrices[4],
        matrices[5],
        matrices[6],
        norm_grads[0],
        norm_grads[1],
        norm_grads[2],
        norm_grads[3],
    )


def solution(mesh):
    placed = (
        P(("wide", "narrow"), None),
        P(("wide", "narrow"), None),
        P("wide", None),
        P(None, "narrow"),
        P(None, "narrow"),
        P(None, "narrow"),
        P("narrow", None),
        P(None, "narrow"),
        P(None, "narrow"),
        P("narrow", None),
        P(),
        P(),
        P(),
        P(),
    )
    return jax.shard_map(
        per_device,
        mesh=mesh,
        in_specs=placed,
        out_specs=(
            P(("wide", "narrow"), None),
            P(("wide", "narrow"), None),
            P(None, "narrow"),
            P(None, "narrow"),
            P(None, "narrow"),
            P("narrow", None),
            P(None, "narrow"),
            P(None, "narrow"),
            P("narrow", None),
            P(),
            P(),
            P(),
            P(),
        ),
        check_vma=False,
    )
```

profile of v0, /device:TPU:0, one launch (start us, length us, event | category | flops | bytes accessed | tf_op | source)
XLA Modules:
  0.0 550.6 jit_solution(14009956408082012891)
XLA Ops:
  10.9 41.9 %all-gather.3.cloned.1.call-done = bf16[768,1024]{1,0:T(8,128)(2,1)} async-done(((bf16[96,1024]{1,0:T(8,128)(2,1)}), bf16[768,1024]{1,0:T(8,128)(2,1)}) %all-gather.3.cloned.1.call-update) | async-done | bytes 1572880 | tf_op jit(solution)/shard_map/all_gather | solution.py:241
  54.6 2.0 fusion.4
  66.2 77.9 %all-reduce.8.cloned.1.call-done = bf16[768,1024]{1,0:T(8,128)(2,1)} async-done(((bf16[768,1024]{1,0:T(8,128)(2,1)}), bf16[768,1024]{1,0:T(8,128)(2,1)}) %all-reduce.8.cloned.1.call-update) | async-done | bytes 1572880 | tf_op jit(solution)/shard_map/psum | solution.py:250
  144.1 2.0 fusion.28
  146.9 3.6 add_convert_fusion.2
  150.4 2.1 fusion.32
  152.6 2.1 fusion.33
  154.7 31.3 %all-gather.5.cloned.1.call-done = bf16[768,1024]{1,0:T(8,128)(2,1)} async-done(((bf16[96,1024]{1,0:T(8,128)(2,1)}), bf16[768,1024]{1,0:T(8,128)(2,1)}) %all-gather.5.cloned.1.call-update) | async-done | bytes 1572880 | tf_op jit(solution)/shard_map/all_gather | solution.py:242
  185.9 5.0 multiply_convert_fusion.1
  192.7 2.2 add_convert_fusion.1
  195.2 3.3 convolution_convert_fusion
  198.4 75.3 %all-reduce.10.cloned.1.call-done = bf16[768,1024]{1,0:T(8,128)(2,1)} async-done(((bf16[768,1024]{1,0:T(8,128)(2,1)}), bf16[768,1024]{1,0:T(8,128)(2,1)}) %all-reduce.10.cloned.1.call-update) | async-done | bytes 1572880 | tf_op jit(solution)/shard_map/psum | solution.py:263
  273.7 3.2 multiply_reduce_fusion.4
  277.5 2.6 multiply_add_fusion
  288.8 3.7 convolution_convert_fusion.3
  292.6 2.0 convolution_convert_fusion.4
  294.6 2.0 convolution_convert_fusion.2
  301.8 3.4 convert_element_type.182
  305.2 73.7 %all-reduce.14.cloned.1.call-done = (bf16[768,1024]{1,0:T(8,128)(2,1)}, bf16[768,1024]{1,0:T(8,128)(2,1)}) async-done(((bf16[768,1024]{1,0:T(8,128)(2,1)}, bf16[768,1024]{1,0:T(8,128)(2,1)}), (bf16[768,1024]{1,0:T(8,128)(2,1)}, bf16[768,1024]{1,0:T(8,128)(2,1)})) %all-reduce.14.cloned.1.call-update) | async-done | bytes 3145744 | tf_op jit(solution)/shard_map/psum | solution.py:256
  378.9 1.9 convert_element_type.192
  382.2 2.2 dynamic-slice_reduce_fusion
  384.4 65.4 %all-reduce = (f32[1024]{0:T(1024)}, f32[1024]{0:T(1024)}, f32[1024]{0:T(1024)}, f32[1024]{0:T(1024)}) all-reduce(f32[1024]{0:T(1024)S(1)} %get-tuple-element.113, f32[1024]{0:T(1024)S(1)} %get-tuple-element.114, f32[1024]{0:T(1024)S(1)} %get-tuple-element.55, ...), channel_id=1, replica_groups=mesh['wide'=16,'narrow'=8] {'wide','narrow'}, use_global_device_ids=true, to_apply=%region_24.25 | all-reduce | flops 4096 | bytes 32768 | tf_op jit(solution)/shard_map/psum | solution.py:301
  451.6 82.6 %all-reduce.12.cloned.1.call-done = (bf16[1024,128]{1,0:T(8,128)(2,1)}, bf16[1024,128]{1,0:T(8,128)(2,1)}, bf16[1024,128]{1,0:T(8,128)(2,1)}, bf16[128,1024]{1,0...) async-done(((bf16[1024,128]{1,0:T(8,128)(2,1)}, bf16[1024,128]{1,0:T(8,128)(2,1)}, bf16[1024,128]{1,0:T(8,128)(2,1)}, ...) | async-done | bytes 4194320 | tf_op jit(solution)/shard_map/psum | solution.py:293
  534.2 3.0 convert_element_type.202
  (177 shorter events, 41.7 us)
Async XLA Ops:
  7.2 178.8 %copy-start = (bf16[512,1024]{1,0:T(8,128)(2,1)S(1)}, bf16[512,1024]{1,0:T(8,128)(2,1)}, u32[]{:S(2)}) copy-start(bf16[512,1024]{1,0:T(8,128)(2,1)} %param.23) | copy-start | bytes 3145732
  7.2 49.4 %copy-start.49 = (f32[1024]{0:T(1024)S(1)}, f32[1024]{0:T(1024)}, u32[]{:S(2)}) copy-start(f32[1024]{0:T(1024)} %param.24) | copy-start | bytes 12292
  7.2 49.4 %copy-start.50 = (f32[1024]{0:T(1024)S(1)}, f32[1024]{0:T(1024)}, u32[]{:S(2)}) copy-start(f32[1024]{0:T(1024)} %param.25) | copy-start | bytes 12292
  7.2 45.6 %all-gather.3.cloned.1.call-start = ((), (), s32[]{:S(2)}) async-start(), calls=%async_computation | async-start | bytes 1769472 | tf_op jit(solution)/shard_map/all_gather | solution.py:241
  8.0 136.2 %all-reduce.8.cloned.1.call-start = ((), (), s32[]{:S(2)}) async-start(), calls=%async_computation.1 | async-start | bytes 3145728 | tf_op jit(solution)/shard_map/psum | solution.py:250
  9.7 49.7 %copy-start.26 = (f32[768,32]{0,1:T(8,128)}, f32[768,32]{0,1:T(8,128)S(1)}, u32[]{:S(2)}) copy-start(f32[768,32]{0,1:T(8,128)S(1)} %get-tuple-element.107) | copy-start | bytes 294916
  10.9 46.4 %copy-start.22 = (bf16[1024,128]{1,0:T(8,128)(2,1)S(1)}, bf16[1024,128]{1,0:T(8,128)(2,1)}, u32[]{:S(2)}) copy-start(bf16[1024,128]{1,0:T(8,128)(2,1)} %param.17) | copy-start | bytes 786436
  52.8 3.9 copy-start.2
  65.2 120.7 %all-gather.5.cloned.1.call-start = ((), (), s32[]{:S(2)}) async-start(), calls=%async_computation.2 | async-start | bytes 1769472 | tf_op jit(solution)/shard_map/all_gather | solution.py:242
  66.0 80.9 %copy-start.48 = (f32[1024]{0:T(1024)S(1)}, f32[1024]{0:T(1024)}, u32[]{:S(2)}) copy-start(f32[1024]{0:T(1024)} %param.26) | copy-start | bytes 12292
  66.0 80.9 %copy-start.51 = (f32[1024]{0:T(1024)S(1)}, f32[1024]{0:T(1024)}, u32[]{:S(2)}) copy-start(f32[1024]{0:T(1024)} %param.27) | copy-start | bytes 12292
  66.0 207.7 %all-reduce.10.cloned.1.call-start = ((), (), s32[]{:S(2)}) async-start(), calls=%async_computation.3 | async-start | bytes 3145728 | tf_op jit(solution)/shard_map/psum | solution.py:263
  185.9 5.0 copy-start.16
  194.9 184.0 %all-reduce.14.cloned.1.call-start = ((), (), s32[]{:S(2)}) async-start(), calls=%async_computation.5 | async-start | bytes 6291456 | tf_op jit(solution)/shard_map/psum | solution.py:256
  273.7 3.8 copy-start.9
  273.7 7.0 %slice-start = ((s8[4718592]{0:T(1024)(128)(4,1)}), s8[4194304]{0:T(1024)(128)(4,1)S(1)}, s32[]{:S(2)}) async-start(s8[4718592]{0:T(1024)(128)(4,1)} %bitcast.74), calls=%async_computation.6 | async-start | bytes 8388608
  288.5 4.1 copy-start.29
  288.5 245.7 %all-reduce.12.cloned.1.call-start = ((), (), s32[]{:S(2)}) async-start(), calls=%async_computation.4 | async-start | bytes 8388608 | tf_op jit(solution)/shard_map/psum | solution.py:293
  296.6 4.0 copy-start.7
  296.6 4.0 copy-start.32
  534.2 4.6 copy-start.19
  537.2 4.0 copy-start.46
  538.8 4.1 copy-start.44
  538.8 4.9 copy-start.1
  (37 other events, 73.3 us)
Sparse Core Ops, SparseCore 0:
  9.7 43.0 all-gather.2
  65.4 78.7 all-reduce.7
  145.8 40.1 all-gather.4
  195.0 78.6 all-reduce.9
  288.6 90.2 all-reduce.13
  382.4 151.7 all-reduce.11
where the time goes:
time: 551 us
  waiting for transfers between devices  384 us (70%)
  blocking collectives  65.4 us (12%)
  other arithmetic  41.2 us (7%)
  matrix products  41 us (7%)
  between operations  14.8 us (3%)
    psum x1, waiting for transfers between devices, per_device(): lax.psum(grad_query.astype(jnp.bfloat16), 'wide').astype(jnp.float32)  82.6 us
    psum x1, waiting for transfers between devices, per_device(): lax.psum(jnp.dot(attended, w_out, preferred_element_type=jnp.float32).ast...  77.9 us
    psum x1, waiting for transfers between devices, per_device(): lax.psum(partial_two.astype(jnp.bfloat16), 'narrow').astype(jnp.float32)  75.3 us
    psum x1, waiting for transfers between devices, per_device(): lax.psum(jnp.dot(hidden, w_down, preferred_element_type=jnp.float32).asty...  73.7 us
    psum x1, blocking collectives, per_device(): lax.psum((jnp.sum(own_one_grad * own_scaled_one, axis=0), jnp.sum(own_one...  65.4 us
    all_gather x1, waiting for transfers between devices, per_device(): lax.all_gather(tokens, 'narrow', axis=0, tiled=True)  41.9 us
    all_gather x1, waiting for transfers between devices, per_device(): lax.all_gather(cotangent, 'narrow', axis=0, tiled=True)  31.3 us
    dot_general x7, matrix products, contract_first(): lax.dot_general(left_side, right_side, (((0,), (0,)), ((), ())), preferre...  12.8 us
  transfers between devices with their start and end apart: 6, of which 6 were waited for; matrix products, arithmetic and copies ran while one was open for 7% of the time, Pallas kernels for 0%

commit v1 on v0

--- a/solution.py
+++ b/solution.py
@@ -290,7 +290,9 @@
     )
     own_scaled_one = lax.dynamic_slice_in_dim(scaled_one, narrow_index * shard_rows, shard_rows, 0)
     matrices = (
-        lax.psum(grad_query.astype(jnp.bfloat16), "wide").astype(jnp.float32),
+        jnp.sum(lax.all_gather(grad_query.astype(jnp.bfloat16), "wide"), axis=0).astype(
+            jnp.float32
+        ),
         lax.psum(grad_key.astype(jnp.bfloat16), "wide").astype(jnp.float32),
         lax.psum(grad_value.astype(jnp.bfloat16), "wide").astype(jnp.float32),
         lax.psum(grad_out.astype(jnp.bfloat16), "wide").astype(jnp.float32),

time: 551 us -> 605 us (1.098)
  waiting for transfers between devices: 384 us -> 430 us
    all_gather x0 -> x1, waiting for transfers between devices: none -> 48.3 us  [per_device(): lax.all_gather(grad_query.astype(jnp.bfloat16), 'wide')]
  transfers between devices with their start and end apart: 6 -> 7, of which waited for: 6 -> 7; matrix products, arithmetic and copies ran while one was open for 7% -> 9% of each run, Pallas kernels for 0% -> 0%
where the time goes in v1:
time: 605 us; the launch traced here: 604 us
  waiting for transfers between devices  430 us (71%)
  blocking collectives  65.2 us (11%)
  other arithmetic  46.7 us (8%)
  matrix products  42.6 us (7%)
  between operations  14.8 us (2%)
    psum x1, waiting for transfers between devices, per_device(): lax.psum(grad_key.astype(jnp.bfloat16), 'wide').astype(jnp.float32)  81.8 us
    psum x1, waiting for transfers between devices, per_device(): lax.psum(jnp.dot(attended, w_out, preferred_element_type=jnp.float32).ast...  77.9 us
    psum x1, waiting for transfers between devices, per_device(): lax.psum(partial_two.astype(jnp.bfloat16), 'narrow').astype(jnp.float32)  75.3 us
    psum x1, waiting for transfers between devices, per_device(): lax.psum(jnp.dot(hidden, w_down, preferred_element_type=jnp.float32).asty...  72.6 us
    psum x1, blocking collectives, per_device(): lax.psum((jnp.sum(own_one_grad * own_scaled_one, axis=0), jnp.sum(own_one...  65.2 us
    all_gather x1, waiting for transfers between devices, per_device(): lax.all_gather(grad_query.astype(jnp.bfloat16), 'wide')  48.3 us
    all_gather x1, waiting for transfers between devices, per_device(): lax.all_gather(tokens, 'narrow', axis=0, tiled=True)  41.2 us
    all_gather x1, waiting for transfers between devices, per_device(): lax.all_gather(cotangent, 'narrow', axis=0, tiled=True)  31.3 us
  transfers between devices with their start and end apart: 7, of which 7 were waited for; matrix products, arithmetic and copies ran while one was open for 9% of the time, Pallas kernels for 0%

profile of v1, /device:TPU:0, one launch (start us, length us, event | category | flops | bytes accessed | tf_op | source)
XLA Modules:
  0.0 603.5 jit_solution(15980570187241223353)
XLA Ops:
  11.5 41.2 %all-gather.5.cloned.1.call-done = bf16[768,1024]{1,0:T(8,128)(2,1)} async-done(((bf16[96,1024]{1,0:T(8,128)(2,1)}), bf16[768,1024]{1,0:T(8,128)(2,1)}) %all-gather.5.cloned.1.call-update) | async-done | bytes 1572880 | tf_op jit(solution)/shard_map/all_gather | solution.py:241
  54.6 2.0 fusion.4
  66.2 77.9 %all-reduce.8.cloned.1.call-done = bf16[768,1024]{1,0:T(8,128)(2,1)} async-done(((bf16[768,1024]{1,0:T(8,128)(2,1)}), bf16[768,1024]{1,0:T(8,128)(2,1)}) %all-reduce.8.cloned.1.call-update) | async-done | bytes 1572880 | tf_op jit(solution)/shard_map/psum | solution.py:250
  144.2 2.0 fusion.28
  147.0 3.5 add_convert_fusion.2
  150.5 2.1 fusion.33
  152.6 2.1 fusion.32
  154.7 31.3 %all-gather.7.cloned.1.call-done = bf16[768,1024]{1,0:T(8,128)(2,1)} async-done(((bf16[96,1024]{1,0:T(8,128)(2,1)}), bf16[768,1024]{1,0:T(8,128)(2,1)}) %all-gather.7.cloned.1.call-update) | async-done | bytes 1572880 | tf_op jit(solution)/shard_map/all_gather | solution.py:242
  186.0 5.0 multiply_convert_fusion.1
  192.8 2.2 add_convert_fusion.1
  195.3 3.3 convolution_convert_fusion
  198.5 75.3 %all-reduce.10.cloned.1.call-done = bf16[768,1024]{1,0:T(8,128)(2,1)} async-done(((bf16[768,1024]{1,0:T(8,128)(2,1)}), bf16[768,1024]{1,0:T(8,128)(2,1)}) %all-reduce.10.cloned.1.call-update) | async-done | bytes 1572880 | tf_op jit(solution)/shard_map/psum | solution.py:263
  273.9 3.2 multiply_reduce_fusion.4
  277.6 2.6 multiply_add_fusion
  288.7 3.8 convolution_convert_fusion.3
  292.5 2.0 convolution_convert_fusion.4
  294.6 2.0 convolution_convert_fusion.2
  300.7 2.7 convolution_convert_fusion.8
  306.4 72.6 %all-reduce.14.cloned.1.call-done = (bf16[768,1024]{1,0:T(8,128)(2,1)}, bf16[768,1024]{1,0:T(8,128)(2,1)}) async-done(((bf16[768,1024]{1,0:T(8,128)(2,1)}, bf16[768,1024]{1,0:T(8,128)(2,1)}), (bf16[768,1024]{1,0:T(8,128)(2,1)}, bf16[768,1024]{1,0:T(8,128)(2,1)})) %all-reduce.14.cloned.1.call-update) | async-done | bytes 3145744 | tf_op jit(solution)/shard_map/psum | solution.py:256
  384.3 65.2 %all-reduce = (f32[1024]{0:T(1024)}, f32[1024]{0:T(1024)}, f32[1024]{0:T(1024)}, f32[1024]{0:T(1024)}) all-reduce(f32[1024]{0:T(1024)S(1)} %get-tuple-element.57, f32[1024]{0:T(1024)S(1)} %get-tuple-element.56, f32[1024]{0:T(1024)S(1)} %get-tuple-element.55, ...), channel_id=1, replica_groups=mesh['wide'=16,'narrow'=8] {'wide','narrow'}, use_global_device_ids=true, to_apply=%region_24.25 | all-reduce | flops 4096 | bytes 32768 | tf_op jit(solution)/shard_map/psum | solution.py:303
  451.3 81.8 %all-reduce.12.cloned.1.call-done = (bf16[1024,128]{1,0:T(8,128)(2,1)}, bf16[1024,128]{1,0:T(8,128)(2,1)}, bf16[128,1024]{1,0:T(8,128)(2,1)}, bf16[1024,512]{1,0...) async-done(((bf16[1024,128]{1,0:T(8,128)(2,1)}, bf16[1024,128]{1,0:T(8,128)(2,1)}, bf16[128,1024]{1,0:T(8,128)(2,1)}, bf16[1024,512]{1,0:T(8,128)(2,1)}, ...) | async-done | bytes 3932176 | tf_op jit(solution)/shard_map/psum | solution.py:296
  538.6 2.9 convert_element_type.204
  544.7 48.3 %all-gather.9.cloned.1.call-done = bf16[16384,128]{1,0:T(8,128)(2,1)} async-done(((bf16[1024,128]{1,0:T(8,128)(2,1)}), bf16[16384,128]{1,0:T(8,128)(2,1)}) %all-gather.9.cloned.1.call-update) | async-done | bytes 4194320 | tf_op jit(solution)/shard_map/all_gather | solution.py:293
  593.0 2.9 reduce_sum.150
  (173 shorter events, 50.7 us)
Async XLA Ops:
  7.2 178.8 %copy-start = (bf16[512,1024]{1,0:T(8,128)(2,1)S(1)}, bf16[512,1024]{1,0:T(8,128)(2,1)}, u32[]{:S(2)}) copy-start(bf16[512,1024]{1,0:T(8,128)(2,1)} %param.23) | copy-start | bytes 3145732
  7.2 49.4 %copy-start.45 = (f32[1024]{0:T(1024)S(1)}, f32[1024]{0:T(1024)}, u32[]{:S(2)}) copy-start(f32[1024]{0:T(1024)} %param.24) | copy-start | bytes 12292
  7.2 49.4 %copy-start.46 = (f32[1024]{0:T(1024)S(1)}, f32[1024]{0:T(1024)}, u32[]{:S(2)}) copy-start(f32[1024]{0:T(1024)} %param.25) | copy-start | bytes 12292
  7.2 45.6 %all-gather.5.cloned.1.call-start = ((), (), s32[]{:S(2)}) async-start(), calls=%async_computation | async-start | bytes 1769472 | tf_op jit(solution)/shard_map/all_gather | solution.py:241
  8.0 136.2 %all-reduce.8.cloned.1.call-start = ((), (), s32[]{:S(2)}) async-start(), calls=%async_computation.1 | async-start | bytes 3145728 | tf_op jit(solution)/shard_map/psum | solution.py:250
  11.5 45.8 %copy-start.24 = (bf16[1024,128]{1,0:T(8,128)(2,1)S(1)}, bf16[1024,128]{1,0:T(8,128)(2,1)}, u32[]{:S(2)}) copy-start(bf16[1024,128]{1,0:T(8,128)(2,1)} %param.19) | copy-start | bytes 786436
  52.8 3.9 copy-start.2
  54.6 3.4 copy-start.21
  65.3 120.8 %all-gather.7.cloned.1.call-start = ((), (), s32[]{:S(2)}) async-start(), calls=%async_computation.2 | async-start | bytes 1769472 | tf_op jit(solution)/shard_map/all_gather | solution.py:242
  66.0 80.9 %copy-start.44 = (f32[1024]{0:T(1024)S(1)}, f32[1024]{0:T(1024)}, u32[]{:S(2)}) copy-start(f32[1024]{0:T(1024)} %param.26) | copy-start | bytes 12292
  66.0 80.9 %copy-start.47 = (f32[1024]{0:T(1024)S(1)}, f32[1024]{0:T(1024)}, u32[]{:S(2)}) copy-start(f32[1024]{0:T(1024)} %param.27) | copy-start | bytes 12292
  66.0 207.8 %all-reduce.10.cloned.1.call-start = ((), (), s32[]{:S(2)}) async-start(), calls=%async_computation.3 | async-start | bytes 3145728 | tf_op jit(solution)/shard_map/psum | solution.py:263
  146.9 3.5 copy-start.17
  186.0 5.0 copy-start.16
  195.0 184.1 %all-reduce.14.cloned.1.call-start = ((), (), s32[]{:S(2)}) async-start(), calls=%async_computation.6 | async-start | bytes 6291456 | tf_op jit(solution)/shard_map/psum | solution.py:256
  273.8 3.8 copy-start.9
  273.9 7.0 %slice-start = ((s8[4718592]{0:T(1024)(128)(4,1)}), s8[4194304]{0:T(1024)(128)(4,1)S(1)}, s32[]{:S(2)}) async-start(s8[4718592]{0:T(1024)(128)(4,1)} %bitcast.75), calls=%async_computation.7 | async-start | bytes 8388608
  288.6 3.9 copy-start.29
  288.7 244.5 %all-reduce.12.cloned.1.call-start = ((), (), s32[]{:S(2)}) async-start(), calls=%async_computation.5 | async-start | bytes 7864320 | tf_op jit(solution)/shard_map/psum | solution.py:296
  288.7 3.8 copy-start.14
  300.4 292.6 %all-gather.9.cloned.1.call-start = ((), (), s32[]{:S(2)}) async-start(), calls=%async_computation.4 | async-start | bytes 4456448 | tf_op jit(solution)/shard_map/all_gather | solution.py:293
  533.1 8.4 %copy-start.20 = (bf16[1024,512]{1,0:T(8,128)(2,1)S(1)}, bf16[1024,512]{1,0:T(8,128)(2,1)}, u32[]{:S(2)}) copy-start(bf16[1024,512]{1,0:T(8,128)(2,1)} %get-tuple-element.80) | copy-start | bytes 3145732
  538.6 4.5 copy-start.19
  543.1 53.6 %copy-start.1 = (bf16[512,1024]{1,0:T(8,128)(2,1)S(1)}, bf16[512,1024]{1,0:T(8,128)(2,1)}, u32[]{:S(2)}) copy-start(bf16[512,1024]{1,0:T(8,128)(2,1)} %param.23) | copy-start | bytes 3145732
  (34 other events, 63.2 us)
Sparse Core Ops, SparseCore 0:
  9.7 43.0 all-gather.4
  65.4 78.7 all-reduce.7
  145.8 40.1 all-gather.6
  195.1 78.7 all-reduce.9
  288.8 90.2 all-reduce.13
  382.5 150.6 all-reduce.11
  536.4 56.5 all-gather.8
